TPU v7x, 32 devices: a whole 2x2x4 slice. The times are simulated.
32 devices in a mesh: seq: 16 (over z, y, core), dp: 2 (over x).
Axes of the slice: x: 2, y: 2, z: 4, core: 2. Of those that a mesh axis runs over, the one named last changes fastest.
Arguments:
- queries: bfloat16 [2, 2048, 1024], P('dp', 'seq'), may hold values from -6 to 6
- keys: bfloat16 [2, 2048, 1024], P('dp', 'seq'), may hold values from -6 to 6
- values: bfloat16 [2, 2048, 1024], P('dp', 'seq'), may hold values from -6 to 6
- d_out: bfloat16 [2, 2048, 1024], P('dp', 'seq'), may hold values from -6 to 6
- segment_ids: int32 [2, 2048], P('dp', 'seq'), may hold values from 0 to 2, never falling along the last dimension, each value on 1 to 1536 neighbouring positions
- block_bucket: int32 [2, 16], P('dp', 'seq'), may hold values from 0 to 63
- block_mask: int32 [2, 16, 5, 1], P('dp', 'seq'), may hold values 0 or 1
- bias_table: bfloat16 [16, 64, 64], replicated, may hold values from -4 to 4
Outputs:
- attention_out: bfloat16 [2, 2048, 1024], P('dp', 'seq')
- d_queries: bfloat16 [2, 2048, 1024], P('dp', 'seq')
- d_keys: bfloat16 [2, 2048, 1024], P('dp', 'seq')
- d_values: bfloat16 [2, 2048, 1024], P('dp', 'seq')
- d_table: float32 [16, 64, 64], replicated
Inputs may be any that keep to these rules, and one draw needn't show every extreme that they name: `segment_ids`: each document is a run of consecutive tokens of one sequence.
All inputs are finite; a program needn't handle non-finite values. No bound on the sum of `block_mask` on one device may be relied on, other than what follows from the above.
Results may differ from a plain program's by a relative error of at most 0.024.
Values may be sent and summed in bfloat16 or wider, within the bound.
No kernel may reach another device: no remote copies, remote signals or barrier semaphores. Data moves between devices by JAX's collectives and lax.ppermute only.
A program may use at most 64 MiB of HBM per device.

v0:
```python
import jax
import jax.numpy as jnp
from jax import lax
from jax.sharding import PartitionSpec as P

H = 16
DH = 64
NB = 64
BLK = 128
masked_value = -1e30


def from_partner(value, axis, apart):
    mask = 2**apart
    pairs = [(source, source ^ mask) for source in range(lax.axis_size(axis))]
    return lax.ppermute(value, axis, pairs)


def expand_blocks(bias_block, row_count, col_count):
    leading = bias_block.shape[:-2]
    row_blocks = bias_block.shape[-2]
    col_blocks = bias_block.shape[-1]
    widened = jnp.broadcast_to(
        bias_block[..., :, None, :, None],
        leading + (row_blocks, row_count // row_blocks, col_blocks, col_count // col_blocks),
    )
    return widened.reshape(leading + (row_count, col_count))


def one_hot_rows(buckets):
    levels_all = jnp.arange(NB, dtype=jnp.float32)
    return (buckets.astype(jnp.float32)[:, None] == levels_all[None, :]).astype(jnp.bfloat16)


def bias_tile(bias_table, row_hot, col_hot):
    picked = jnp.einsum(
        "bn,hnm->hbm", row_hot, bias_table, preferred_element_type=jnp.float32
    ).astype(jnp.bfloat16)
    return jnp.einsum("hbm,cm->hbc", picked, col_hot, preferred_element_type=jnp.float32)


def allowed_pairs(seg_rows, seg_cols, block_ok):
    same_doc = seg_rows.astype(jnp.float32)[:, None] == seg_cols.astype(jnp.float32)[None, :]
    return same_doc & expand_blocks(block_ok, seg_rows.shape[0], seg_cols.shape[0])


def masked_scores(query_heads, key_heads, bias_block, allowed):
    products = jnp.einsum(
        "thd,uhd->htu", query_heads, key_heads, preferred_element_type=jnp.float32
    )
    shifted = products * 0.125 + expand_blocks(bias_block, query_heads.shape[0], key_heads.shape[0])
    return jnp.where(allowed[None], shifted, masked_value)


def grad_terms(scores, allowed, lse, row_delta, grad_heads, value_heads):
    probs = jnp.where(allowed[None], jnp.exp(scores - lse[:, :, None]), 0.0)
    dprob = jnp.einsum("thd,uhd->htu", grad_heads, value_heads, preferred_element_type=jnp.float32)
    dscore = probs * (dprob - row_delta[:, :, None])
    return (probs.astype(jnp.bfloat16), dscore)


def local(queries, keys, values, d_out, segment_ids, block_bucket, block_mask, bias_table):
    row_count = queries.shape[1]
    block_count = row_count // BLK
    level_count = lax.axis_size("seq").bit_length() - 1
    query_heads = queries[0].reshape(row_count, H, DH)
    grad_heads = d_out[0].reshape(row_count, H, DH)
    own_keys = keys[0]
    own_values = values[0]
    own_seg = segment_ids[0]
    own_bucket = block_bucket[0]
    own_mask = block_mask[0] != 0
    own_hot = one_hot_rows(own_bucket)
    own_hot_wide = own_hot.astype(jnp.float32)
    section_list = list(range(level_count + 1))
    stored = {}
    run_max = jnp.full((H, row_count), masked_value, jnp.float32)
    run_sum = jnp.zeros((H, row_count), jnp.float32)
    run_acc = jnp.zeros((row_count, H, DH), jnp.float32)
    for section_num in section_list:
        if section_num == 0:
            key_rows, value_rows, seg_cols, bucket_cols = (
                own_keys,
                own_values,
                own_seg,
                own_bucket,
            )
            block_ok = own_mask[:, 0, :] | jnp.eye(block_count, dtype=bool)
        else:
            key_rows, value_rows, seg_cols, bucket_cols = from_partner(
                (
                    own_keys,
                    own_values,
                    own_seg.astype(jnp.bfloat16),
                    own_bucket.astype(jnp.bfloat16),
                ),
                "seq",
                section_num - 1,
            )
            block_ok = own_mask[:, section_num, :]
        key_heads = key_rows.reshape(row_count, H, DH)
        value_heads = value_rows.reshape(row_count, H, DH)
        col_hot = one_hot_rows(bucket_cols)
        bias_block = bias_tile(bias_table, own_hot, col_hot)
        allowed = allowed_pairs(own_seg, seg_cols, block_ok)
        stored[section_num] = (key_heads, value_heads, seg_cols, col_hot, bias_block, allowed)
        scores = masked_scores(query_heads, key_heads, bias_block, allowed)
        fresh_max = jnp.maximum(run_max, jnp.max(scores, axis=-1))
        rescale = jnp.exp(run_max - fresh_max)
        weights = jnp.where(allowed[None], jnp.exp(scores - fresh_max[:, :, None]), 0.0)
        run_sum = run_sum * rescale + jnp.sum(weights, axis=-1)
        run_acc = run_acc * rescale.T[:, :, None] + jnp.einsum(
            "htu,uhd->thd",
            weights.astype(jnp.bfloat16),
            value_heads,
            preferred_element_type=jnp.float32,
        )
        run_max = fresh_max
    out_heads = (run_acc / run_sum.T[:, :, None]).astype(jnp.bfloat16)
    lse = run_max + jnp.log(run_sum)
    row_delta = jnp.sum(out_heads.astype(jnp.float32) * grad_heads.astype(jnp.float32), axis=-1).T
    out_rows = out_heads.reshape(row_count, H * DH)
    query_acc = jnp.zeros((row_count, H, DH), jnp.float32)
    key_acc = jnp.zeros((row_count, H, DH), jnp.float32)
    value_acc = jnp.zeros((row_count, H, DH), jnp.float32)
    table_acc = jnp.zeros((H, NB, NB), jnp.float32)
    for section_num in section_list:
        key_heads, value_heads, seg_cols, col_hot, bias_block, allowed = stored[section_num]
        scores = masked_scores(query_heads, key_heads, bias_block, allowed)
        probs_low, dscore = grad_terms(scores, allowed, lse, row_delta, grad_heads, value_heads)
        dscore_low = dscore.astype(jnp.bfloat16)
        query_acc = (
            query_acc
            + jnp.einsum("htu,uhd->thd", dscore_low, key_heads, preferred_element_type=jnp.float32)
            * 0.125
        )
        block_sums = dscore.reshape(H, block_count, BLK, block_count, BLK).sum(axis=(2, 4))
        table_acc = table_acc + jnp.einsum(
            "bn,hbc,cm->hnm",
            own_hot_wide,
            block_sums,
            col_hot.astype(jnp.float32),
            precision=lax.Precision.HIGHEST,
        )
        if section_num == 0:
            key_acc = (
                jnp.einsum(
                    "htu,thd->uhd", dscore_low, query_heads, preferred_element_type=jnp.float32
                )
                * 0.125
            )
            value_acc = jnp.einsum(
                "htu,thd->uhd", probs_low, grad_heads, preferred_element_type=jnp.float32
            )
        else:
            key_term = (
                jnp.einsum(
                    "htu,thd->uhd", dscore_low, query_heads, preferred_element_type=jnp.float32
                )
                * 0.125
            ).astype(jnp.bfloat16)
            value_term = jnp.einsum(
                "htu,thd->uhd", probs_low, grad_heads, preferred_element_type=jnp.float32
            ).astype(jnp.bfloat16)
            back_keys, back_values = from_partner(
                (key_term.reshape(row_count, H * DH), value_term.reshape(row_count, H * DH)),
                "seq",
                section_num - 1,
            )
            key_acc = key_acc + back_keys.reshape(row_count, H, DH).astype(jnp.float32)
            value_acc = value_acc + back_values.reshape(row_count, H, DH).astype(jnp.float32)
    table_total = lax.psum(table_acc, ("seq", "dp"))
    feature_count = H * DH
    return (
        out_rows.reshape(1, row_count, feature_count),
        query_acc.astype(jnp.bfloat16).reshape(1, row_count, feature_count),
        key_acc.astype(jnp.bfloat16).reshape(1, row_count, feature_count),
        value_acc.astype(jnp.bfloat16).reshape(1, row_count, feature_count),
        table_total,
    )


def solution(mesh):
    in_specs = (
        P("dp", "seq", None),
        P("dp", "seq", None),
        P("dp", "seq", None),
        P("dp", "seq", None),
        P("dp", "seq"),
        P("dp", "seq"),
        P("dp", "seq", None, None),
        P(),
    )
    out_specs = (
        P("dp", "seq", None),
        P("dp", "seq", None),
        P("dp", "seq", None),
        P("dp", "seq", None),
        P(),
    )
    return jax.shard_map(local, mesh=mesh, in_specs=in_specs, out_specs=out_specs, check_vma=False)
```

profile of v0, /device:TPU:0, one launch (start us, length us, event | category | flops | bytes accessed | tf_op | source)
XLA Modules:
  0.0 256.8 jit_solution(7733567742736410515)
XLA Ops:
  8.0 3.0 %collective-permute-start.4 = (bf16[128]{0:T(256)(128)(2,1)S(1)}, bf16[128]{0:T(256)(128)(2,1)S(1)}, u32[]{:S(2)}, u32[]{:S(2)}) collective-permute-start(bf16[128]{0:T(256)(128)(2,1)S(1)} %get-tuple-element.40), channel_id=1, source_target_pairs={{0,4},{2,6},{4,0},{6,2},{8,12},{10,14},{12,8},{14,10},{16,20},{18,... | collective-permute-start | bytes 776 | tf_op jit(solution)/shard_map/ppermute | solution.py:16
  10.9 1.6 collective-permute-start.8
  12.5 2.6 %collective-permute-start.12 = (bf16[128]{0:T(256)(128)(2,1)S(1)}, bf16[128]{0:T(256)(128)(2,1)S(1)}, u32[]{:S(2)}, u32[]{:S(2)}) collective-permute-start(bf16[128]{0:T(256)(128)(2,1)S(1)} %get-tuple-element.40), channel_id=1, source_target_pairs={{0,16},{2,18},{4,20},{6,22},{8,24},{10,26},{12,28},{14,30},{16,0},... | collective-permute-start | bytes 776 | tf_op jit(solution)/shard_map/ppermute | solution.py:16
  15.8 1.7 collective-permute-start.14
  23.2 1.8 collective-permute-start.10
  26.7 1.8 collective-permute-start.6
  31.8 2.6 %collective-permute-start.13 = (bf16[128,1024]{1,0:T(8,128)(2,1)}, bf16[128,1024]{1,0:T(8,128)(2,1)S(1)}, u32[]{:S(2)}, u32[]{:S(2)}) collective-permute-start(bf16[128,1024]{1,0:T(8,128)(2,1)} %bitcast.15), channel_id=1, source_target_pairs={{0,16},{2,18},{4,20},{6,22},{8,24},{10,26},{12,28},{14,30},{16,0},... | collective-permute-start | bytes 786440 | tf_op jit(solution)/shard_map/ppermute | solution.py:16
  38.0 2.6 %broadcast_compare_fusion = (pred[128,128]{0,1:T(8,128)(4,1)S(1)}, pred[128,128]{0,1:T(8,128)(4,1)S(1)}, pred[128,128]{0,1:T(8,128)(4,1)S(1)}, pred[128,128]{0,1:T(8,128)(4,1)S(1)}, pred[128,128]{0,1:T(8,128)(4,1)S(1)}) fusion(f32[128]{0:T(128)S(1)} %get-tuple-element.41, pred[]{:T(512)} %bitcast.25, f32[128]{0:T(128)S(1)} %convert_element_type.245, ...), kind=kLoop, calls=%fused_computation.151 | loop fusion | flops 147456 | bytes 84484 | tf_op jit(solution)/shard_map/eq | solution.py:43
  41.1 6.8 %collective-permute-done.13 = bf16[128,1024]{1,0:T(8,128)(2,1)S(1)} collective-permute-done((bf16[128,1024]{1,0:T(8,128)(2,1)}, bf16[128,1024]{1,0:T(8,128)(2,1)S(1)}, u32[]{:S(2)}, u32[]{:S(2)}) %collective-permute-start.13) | collective-permute-done | bytes 262176 | tf_op jit(solution)/shard_map/ppermute | solution.py:16
  51.4 1.8 copy.75
  53.2 2.3 fusion.151
  55.5 1.8 copy.72
  57.3 2.3 fusion.152
  59.6 1.8 copy.69
  61.4 1.5 fusion.153
  66.0 1.8 copy.79
  67.8 2.0 convolution_bitcast_fusion
  69.9 1.8 copy.76
  71.7 2.4 convolution_bitcast_fusion.1
  74.1 1.8 copy.73
  75.8 2.4 convolution_bitcast_fusion.2
  78.3 1.8 copy.70
  80.8 3.1 %multiply_reduce_fusion = (f32[128,16]{0,1:T(8,128)S(1)}, bf16[128,16,64]{0,2,1:T(8,128)(2,1)}) fusion(bf16[128,16,64]{0,2,1:T(8,128)(2,1)S(1)} %bitcast.299, f32[128,16]{0,1:T(8,128)S(1)} %copy-done.24, f32[128,16,64]{0,2,1:T(8,128)} %convolution_bitcast_fusion, f32[128,16]{0,1:T(8,128)S(1)} %copy-done.27, f32[128,16,64]{0,2,1:T(8,128)} %convolution_bitcast_fusion.1, ...), kind=kOutput, calls=%fused_computation.103 | convolution fusion | flops 36042752 | bytes 3997696 | tf_op jit(solution)/shard_map/htu,uhd->thd/dot_general | solution.py:112
  99.8 1.9 copy.102
  106.1 1.9 copy.103
  108.0 2.9 %collective-permute-start.19 = (bf16[128,1024]{0,1:T(8,128)(2,1)}, bf16[128,1024]{0,1:T(8,128)(2,1)}, u32[]{:S(2)}, u32[]{:S(2)}) collective-permute-start(bf16[128,1024]{0,1:T(8,128)(2,1)} %bitcast.353), channel_id=1, source_target_pairs={{0,16},{2,18},{4,20},{6,22},{8,24},{10,26},{12,28},{14,30},{16,0},... | collective-permute-start | bytes 786440 | tf_op jit(solution)/shard_map/ppermute | solution.py:16
  111.7 2.0 collective-permute-start.23
  113.8 1.5 multiply_add_fusion
  115.9 8.2 %collective-permute-done.19 = bf16[128,1024]{0,1:T(8,128)(2,1)} collective-permute-done((bf16[128,1024]{0,1:T(8,128)(2,1)}, bf16[128,1024]{0,1:T(8,128)(2,1)}, u32[]{:S(2)}, u32[]{:S(2)}) %collective-permute-start.19) | collective-permute-done | bytes 262176 | tf_op jit(solution)/shard_map/ppermute | solution.py:16
  127.2 9.0 %collective-permute-done.23 = bf16[128,1024]{0,1:T(8,128)(2,1)S(1)} collective-permute-done((bf16[128,1024]{0,1:T(8,128)(2,1)}, bf16[128,1024]{0,1:T(8,128)(2,1)S(1)}, u32[]{:S(2)}, u32[]{:S(2)}) %collective-permute-start.23) | collective-permute-done | bytes 262176 | tf_op jit(solution)/shard_map/ppermute | solution.py:16
  139.2 108.9 %all-reduce.2.cloned.1.call-done = f32[16,64,64]{2,1,0:T(8,128)} async-done(((f32[16,64,64]{2,1,0:T(8,128)}), f32[16,64,64]{2,1,0:T(8,128)}) %all-reduce.2.cloned.1.call-update) | async-done | bytes 262160 | tf_op jit(solution)/shard_map/psum | solution.py:172
  248.1 1.9 copy.134
  (162 shorter events, 48.1 us)
Async XLA Ops:
  7.2 12.0 %copy-start = (bf16[16,64,64]{2,1,0:T(8,128)(2,1)S(1)}, bf16[16,64,64]{2,1,0:T(8,128)(2,1)}, u32[]{:S(2)}) copy-start(bf16[16,64,64]{2,1,0:T(8,128)(2,1)} %param.15) | copy-start | bytes 393220
  7.2 240.9 %all-reduce.2.cloned.1.call-start = ((), (), s32[]{:S(2)}) async-start(), calls=%async_computation | async-start | bytes 1048576 | tf_op jit(solution)/shard_map/psum | solution.py:172
  8.0 27.9 %collective-permute-start.4 = (bf16[128]{0:T(256)(128)(2,1)S(1)}, bf16[128]{0:T(256)(128)(2,1)S(1)}, u32[]{:S(2)}, u32[]{:S(2)}) collective-permute-start(bf16[128]{0:T(256)(128)(2,1)S(1)} %get-tuple-element.40), channel_id=1, source_target_pairs={{0,4},{2,6},{4,0},{6,2},{8,12},{10,14},{12,8},{14,10},{16,20},{18,... | collective-permute-start | bytes 776 | tf_op jit(solution)/shard_map/ppermute | solution.py:16
  10.9 25.5 %collective-permute-start.8 = (bf16[128]{0:T(256)(128)(2,1)S(1)}, bf16[128]{0:T(256)(128)(2,1)S(1)}, u32[]{:S(2)}, u32[]{:S(2)}) collective-permute-start(bf16[128]{0:T(256)(128)(2,1)S(1)} %get-tuple-element.40), channel_id=1, source_target_pairs={{0,8},{2,10},{4,12},{6,14},{8,0},{10,2},{12,4},{14,6},{16,24},{18,... | collective-permute-start | bytes 776 | tf_op jit(solution)/shard_map/ppermute | solution.py:16
  12.5 25.1 %collective-permute-start.12 = (bf16[128]{0:T(256)(128)(2,1)S(1)}, bf16[128]{0:T(256)(128)(2,1)S(1)}, u32[]{:S(2)}, u32[]{:S(2)}) collective-permute-start(bf16[128]{0:T(256)(128)(2,1)S(1)} %get-tuple-element.40), channel_id=1, source_target_pairs={{0,16},{2,18},{4,20},{6,22},{8,24},{10,26},{12,28},{14,30},{16,0},... | collective-permute-start | bytes 776 | tf_op jit(solution)/shard_map/ppermute | solution.py:16
  15.1 22.5 %collective-permute-start = (bf16[128]{0:T(256)(128)(2,1)S(1)}, bf16[128]{0:T(256)(128)(2,1)S(1)}, u32[]{:S(2)}, u32[]{:S(2)}) collective-permute-start(bf16[128]{0:T(256)(128)(2,1)S(1)} %get-tuple-element.40), channel_id=1, source_target_pairs={{0,2},{2,0},{4,6},{6,4},{8,10},{10,8},{12,14},{14,12},{16,18},{18,... | collective-permute-start | bytes 776 | tf_op jit(solution)/shard_map/ppermute | solution.py:16
  15.8 7.4 %collective-permute-start.14 = (bf16[1]{0:T(256)(128)(2,1)}, bf16[1]{0:T(256)(128)(2,1)}, u32[]{:S(2)}, u32[]{:S(2)}) collective-permute-start(bf16[1]{0:T(256)(128)(2,1)} %bitcast.17), channel_id=1, source_target_pairs={{0,16},{2,18},{4,20},{6,22},{8,24},{10,26},{12,28},{14,30},{16,0},... | collective-permute-start | bytes 14 | tf_op jit(solution)/shard_map/ppermute | solution.py:16
  23.2 3.6 %collective-permute-start.10 = (bf16[1]{0:T(256)(128)(2,1)}, bf16[1]{0:T(256)(128)(2,1)}, u32[]{:S(2)}, u32[]{:S(2)}) collective-permute-start(bf16[1]{0:T(256)(128)(2,1)} %bitcast.17), channel_id=1, source_target_pairs={{0,8},{2,10},{4,12},{6,14},{8,0},{10,2},{12,4},{14,6},{16,24},{18,... | collective-permute-start | bytes 14 | tf_op jit(solution)/shard_map/ppermute | solution.py:16
  26.7 3.5 %collective-permute-start.6 = (bf16[1]{0:T(256)(128)(2,1)}, bf16[1]{0:T(256)(128)(2,1)}, u32[]{:S(2)}, u32[]{:S(2)}) collective-permute-start(bf16[1]{0:T(256)(128)(2,1)} %bitcast.17), channel_id=1, source_target_pairs={{0,4},{2,6},{4,0},{6,2},{8,12},{10,14},{12,8},{14,10},{16,20},{18,... | collective-permute-start | bytes 14 | tf_op jit(solution)/shard_map/ppermute | solution.py:16
  30.2 1.6 collective-permute-start.2
  31.8 16.0 %collective-permute-start.13 = (bf16[128,1024]{1,0:T(8,128)(2,1)}, bf16[128,1024]{1,0:T(8,128)(2,1)S(1)}, u32[]{:S(2)}, u32[]{:S(2)}) collective-permute-start(bf16[128,1024]{1,0:T(8,128)(2,1)} %bitcast.15), channel_id=1, source_target_pairs={{0,16},{2,18},{4,20},{6,22},{8,24},{10,26},{12,28},{14,30},{16,0},... | collective-permute-start | bytes 786440 | tf_op jit(solution)/shard_map/ppermute | solution.py:16
  35.8 14.4 %collective-permute-start.9 = (bf16[128,1024]{1,0:T(8,128)(2,1)}, bf16[128,1024]{1,0:T(8,128)(2,1)}, u32[]{:S(2)}, u32[]{:S(2)}) collective-permute-start(bf16[128,1024]{1,0:T(8,128)(2,1)} %bitcast.15), channel_id=1, source_target_pairs={{0,8},{2,10},{4,12},{6,14},{8,0},{10,2},{12,4},{14,6},{16,24},{18,... | collective-permute-start | bytes 786440 | tf_op jit(solution)/shard_map/ppermute | solution.py:16
  36.4 19.1 %collective-permute-start.5 = (bf16[128,1024]{1,0:T(8,128)(2,1)}, bf16[128,1024]{1,0:T(8,128)(2,1)}, u32[]{:S(2)}, u32[]{:S(2)}) collective-permute-start(bf16[128,1024]{1,0:T(8,128)(2,1)} %bitcast.15), channel_id=1, source_target_pairs={{0,4},{2,6},{4,0},{6,2},{8,12},{10,14},{12,8},{14,10},{16,20},{18,... | collective-permute-start | bytes 786440 | tf_op jit(solution)/shard_map/ppermute | solution.py:16
  37.6 22.0 %collective-permute-start.1 = (bf16[128,1024]{1,0:T(8,128)(2,1)}, bf16[128,1024]{1,0:T(8,128)(2,1)}, u32[]{:S(2)}, u32[]{:S(2)}) collective-permute-start(bf16[128,1024]{1,0:T(8,128)(2,1)} %bitcast.15), channel_id=1, source_target_pairs={{0,2},{2,0},{4,6},{6,4},{8,10},{10,8},{12,14},{14,12},{16,18},{18,... | collective-permute-start | bytes 786440 | tf_op jit(solution)/shard_map/ppermute | solution.py:16
  37.6 28.4 %collective-permute-start.15 = (bf16[128,1024]{1,0:T(8,128)(2,1)}, bf16[128,1024]{1,0:T(8,128)(2,1)}, u32[]{:S(2)}, u32[]{:S(2)}) collective-permute-start(bf16[128,1024]{1,0:T(8,128)(2,1)} %bitcast.22), channel_id=1, source_target_pairs={{0,16},{2,18},{4,20},{6,22},{8,24},{10,26},{12,28},{14,30},{16,0},... | collective-permute-start | bytes 786440 | tf_op jit(solution)/shard_map/ppermute | solution.py:16
  47.8 22.0 %collective-permute-start.11 = (bf16[128,1024]{1,0:T(8,128)(2,1)}, bf16[128,1024]{1,0:T(8,128)(2,1)}, u32[]{:S(2)}, u32[]{:S(2)}) collective-permute-start(bf16[128,1024]{1,0:T(8,128)(2,1)} %bitcast.22), channel_id=1, source_target_pairs={{0,8},{2,10},{4,12},{6,14},{8,0},{10,2},{12,4},{14,6},{16,24},{18,... | collective-permute-start | bytes 786440 | tf_op jit(solution)/shard_map/ppermute | solution.py:16
  50.2 23.9 %collective-permute-start.7 = (bf16[128,1024]{1,0:T(8,128)(2,1)}, bf16[128,1024]{1,0:T(8,128)(2,1)}, u32[]{:S(2)}, u32[]{:S(2)}) collective-permute-start(bf16[128,1024]{1,0:T(8,128)(2,1)} %bitcast.22), channel_id=1, source_target_pairs={{0,4},{2,6},{4,0},{6,2},{8,12},{10,14},{12,8},{14,10},{16,20},{18,... | collective-permute-start | bytes 786440 | tf_op jit(solution)/shard_map/ppermute | solution.py:16
  55.5 22.8 %collective-permute-start.3 = (bf16[128,1024]{1,0:T(8,128)(2,1)}, bf16[128,1024]{1,0:T(8,128)(2,1)}, u32[]{:S(2)}, u32[]{:S(2)}) collective-permute-start(bf16[128,1024]{1,0:T(8,128)(2,1)} %bitcast.22), channel_id=1, source_target_pairs={{0,2},{2,0},{4,6},{6,4},{8,10},{10,8},{12,14},{14,12},{16,18},{18,... | collective-permute-start | bytes 786440 | tf_op jit(solution)/shard_map/ppermute | solution.py:16
  105.1 8.7 %copy-start.30 = (f32[64]{0:T(128)S(1)}, f32[64]{0:T(128)}, u32[]{:S(2)}) copy-start(f32[64]{0:T(128)} %get-tuple-element.69) | copy-start | bytes 772
  105.1 8.7 %copy-start.31 = (f32[64]{0:T(128)S(1)}, f32[64]{0:T(128)}, u32[]{:S(2)}) copy-start(f32[64]{0:T(128)} %get-tuple-element.70) | copy-start | bytes 772
  105.1 8.7 %copy-start.32 = (f32[64]{0:T(128)S(1)}, f32[64]{0:T(128)}, u32[]{:S(2)}) copy-start(f32[64]{0:T(128)} %get-tuple-element.71) | copy-start | bytes 772
  106.1 9.3 %copy-start.7 = (f32[16,128,128]{1,2,0:T(8,128)S(1)}, f32[16,128,128]{1,2,0:T(8,128)}, u32[]{:S(2)}) copy-start(f32[16,128,128]{1,2,0:T(8,128)} %copy-done.5) | copy-start | bytes 3145732
  108.0 16.1 %collective-permute-start.19 = (bf16[128,1024]{0,1:T(8,128)(2,1)}, bf16[128,1024]{0,1:T(8,128)(2,1)}, u32[]{:S(2)}, u32[]{:S(2)}) collective-permute-start(bf16[128,1024]{0,1:T(8,128)(2,1)} %bitcast.353), channel_id=1, source_target_pairs={{0,16},{2,18},{4,20},{6,22},{8,24},{10,26},{12,28},{14,30},{16,0},... | collective-permute-start | bytes 786440 | tf_op jit(solution)/shard_map/ppermute | solution.py:16
  110.9 13.7 %collective-permute-start.18 = (bf16[128,1024]{0,1:T(8,128)(2,1)}, bf16[128,1024]{0,1:T(8,128)(2,1)}, u32[]{:S(2)}, u32[]{:S(2)}) collective-permute-start(bf16[128,1024]{0,1:T(8,128)(2,1)} %bitcast.352), channel_id=1, source_target_pairs={{0,8},{2,10},{4,12},{6,14},{8,0},{10,2},{12,4},{14,6},{16,24},{18,... | collective-permute-start | bytes 786440 | tf_op jit(solution)/shard_map/ppermute | solution.py:16
  110.9 15.0 %collective-permute-start.17 = (bf16[128,1024]{0,1:T(8,128)(2,1)}, bf16[128,1024]{0,1:T(8,128)(2,1)}, u32[]{:S(2)}, u32[]{:S(2)}) collective-permute-start(bf16[128,1024]{0,1:T(8,128)(2,1)} %bitcast.355), channel_id=1, source_target_pairs={{0,4},{2,6},{4,0},{6,2},{8,12},{10,14},{12,8},{14,10},{16,20},{18,... | collective-permute-start | bytes 786440 | tf_op jit(solution)/shard_map/ppermute | solution.py:16
  111.7 14.1 %collective-permute-start.16 = (bf16[128,1024]{0,1:T(8,128)(2,1)}, bf16[128,1024]{0,1:T(8,128)(2,1)}, u32[]{:S(2)}, u32[]{:S(2)}) collective-permute-start(bf16[128,1024]{0,1:T(8,128)(2,1)} %bitcast.354), channel_id=1, source_target_pairs={{0,2},{2,0},{4,6},{6,4},{8,10},{10,8},{12,14},{14,12},{16,18},{18,... | collective-permute-start | bytes 786440 | tf_op jit(solution)/shard_map/ppermute | solution.py:16
  111.7 24.5 %collective-permute-start.23 = (bf16[128,1024]{0,1:T(8,128)(2,1)}, bf16[128,1024]{0,1:T(8,128)(2,1)S(1)}, u32[]{:S(2)}, u32[]{:S(2)}) collective-permute-start(bf16[128,1024]{0,1:T(8,128)(2,1)} %bitcast.343), channel_id=1, source_target_pairs={{0,16},{2,18},{4,20},{6,22},{8,24},{10,26},{12,28},{14,30},{16,0},... | collective-permute-start | bytes 786440 | tf_op jit(solution)/shard_map/ppermute | solution.py:16
  115.4 8.7 %copy-start.21 = (bf16[16,128,64]{1,2,0:T(8,128)(2,1)S(1)}, bf16[16,128,64]{1,2,0:T(8,128)(2,1)}, u32[]{:S(2)}) copy-start(bf16[16,128,64]{1,2,0:T(8,128)(2,1)} %convolution_convert_fusion.1) | copy-start | bytes 786436
  115.4 9.2 %copy-start.20 = (bf16[16,128,64]{1,2,0:T(8,128)(2,1)S(1)}, bf16[16,128,64]{1,2,0:T(8,128)(2,1)}, u32[]{:S(2)}) copy-start(bf16[16,128,64]{1,2,0:T(8,128)(2,1)} %convolution_convert_fusion.2) | copy-start | bytes 786436
  124.1 13.2 %collective-permute-start.22 = (bf16[128,1024]{0,1:T(8,128)(2,1)S(1)}, bf16[128,1024]{0,1:T(8,128)(2,1)S(1)}, u32[]{:S(2)}, u32[]{:S(2)}) collective-permute-start(bf16[128,1024]{0,1:T(8,128)(2,1)S(1)} %bitcast.342), channel_id=1, source_target_pairs={{0,8},{2,10},{4,12},{6,14},{8,0},{10,2},{12,4},{14,6},{16,24},{18,... | collective-permute-start | bytes 786440 | tf_op jit(solution)/shard_map/ppermute | solution.py:16
  124.6 12.7 %collective-permute-start.21 = (bf16[128,1024]{0,1:T(8,128)(2,1)S(1)}, bf16[128,1024]{0,1:T(8,128)(2,1)S(1)}, u32[]{:S(2)}, u32[]{:S(2)}) collective-permute-start(bf16[128,1024]{0,1:T(8,128)(2,1)S(1)} %bitcast.341), channel_id=1, source_target_pairs={{0,4},{2,6},{4,0},{6,2},{8,12},{10,14},{12,8},{14,10},{16,20},{18,... | collective-permute-start | bytes 786440 | tf_op jit(solution)/shard_map/ppermute | solution.py:16
  125.8 11.5 %collective-permute-start.20 = (bf16[128,1024]{0,1:T(8,128)(2,1)S(1)}, bf16[128,1024]{0,1:T(8,128)(2,1)S(1)}, u32[]{:S(2)}, u32[]{:S(2)}) collective-permute-start(bf16[128,1024]{0,1:T(8,128)(2,1)S(1)} %bitcast.345), channel_id=1, source_target_pairs={{0,2},{2,0},{4,6},{6,4},{8,10},{10,8},{12,14},{14,12},{16,18},{18,... | collective-permute-start | bytes 786440 | tf_op jit(solution)/shard_map/ppermute | solution.py:16
  (27 other events, 52.6 us)
Sparse Core Ops, SparseCore 0:
  115.5 132.5 all-reduce.1
where the time goes:
time: 258 us; the launch traced here: 257 us
  waiting for transfers between devices  136 us (53%)
  matrix products  38.1 us (15%)
  local copies, waits for them, and re-layouts  28.9 us (11%)
  starting transfers between devices  26.2 us (10%)
  between operations  17.7 us (7%)
  other arithmetic  9.98 us (4%)
    psum x1, waiting for transfers between devices, local(): table_total = lax.psum(table_acc, ('seq', 'dp'))  109 us
    ppermute x24, waiting for transfers between devices, from_partner(): return lax.ppermute(value, axis, pairs)  27.1 us
    ppermute x24, starting transfers between devices, from_partner(): return lax.ppermute(value, axis, pairs)  26.2 us
    unnamed x77, local copies, waits for them, and re-layouts  14.8 us
    ppermute x8, local copies, waits for them, and re-layouts, from_partner(): return lax.ppermute(value, axis, pairs)  13.4 us
    dot_general x5, matrix products, local(): jnp.einsum('htu,uhd->thd', weights.astype(jnp.bfloat16), value_heads, pre...  11 us
    dot_general x5, matrix products, masked_scores(): jnp.einsum('thd,uhd->htu', query_heads, key_heads, preferred_element_type...  7.82 us
  transfers between devices with their start and end apart: 25, of which 9 were waited for; matrix products, arithmetic and copies ran while one was open for 17% of the time, Pallas kernels for 0%

commit v1 on v0

--- a/solution.py
+++ b/solution.py
@@ -169,7 +169,7 @@
             )
             key_acc = key_acc + back_keys.reshape(row_count, H, DH).astype(jnp.float32)
             value_acc = value_acc + back_values.reshape(row_count, H, DH).astype(jnp.float32)
-    table_total = lax.psum(table_acc, ("seq", "dp"))
+    table_total = jax.lax.all_gather(table_acc, axis_name=("seq", "dp")).sum(axis=0)
     feature_count = H * DH
     return (
         out_rows.reshape(1, row_count, feature_count),

time: 258 us -> 241 us (0.934)
  waiting for transfers between devices: 136 us -> 97 us
  other arithmetic: 9.98 us -> 24.1 us
  matrix products: 38.1 us -> 51.5 us
  local copies, waits for them, and re-layouts: 28.9 us -> 21.6 us
    psum x1 -> x0, waiting for transfers between devices: 109 us -> none  [local(): table_total = lax.psum(table_acc, ('seq', 'dp'))]
    all_gather x0 -> x1, waiting for transfers between devices: none -> 81.5 us  [local(): jax.lax.all_gather(table_acc, axis_name=('seq', 'dp')).sum(axis=0)]
    ppermute x24, waiting for transfers between devices: 27.1 us -> 15.5 us  [from_partner(): return lax.ppermute(value, axis, pairs)]
    reduce_sum x0 -> x1, other arithmetic: none -> 8.66 us  [local(): jax.lax.all_gather(table_acc, axis_name=('seq', 'dp')).sum(axis=0)]
    dot_general x5, matrix products: 4.34 us -> 11.6 us  [grad_terms(): jnp.einsum('thd,uhd->htu', grad_heads, value_heads, preferred_element_typ...]
    unnamed x77 -> x26, local copies, waits for them, and re-layouts: 14.8 us -> 9.96 us
    dot_general x5, matrix products: 4.63 us -> 9.02 us  [local(): jnp.einsum('htu,thd->uhd', probs_low, grad_heads, preferred_element_type=...]
  transfers between devices with their start and end apart: 25 -> 25, of which waited for: 9 -> 7; matrix products, arithmetic and copies ran while one was open for 17% -> 28% of each run, Pallas kernels for 0% -> 0%
where the time goes in v1:
time: 241 us; the launch traced here: 240 us
  waiting for transfers between devices  97 us (40%)
  matrix products  51.5 us (21%)
  starting transfers between devices  27.9 us (12%)
  other arithmetic  24.1 us (10%)
  local copies, waits for them, and re-layouts  21.6 us (9%)
  between operations  17.6 us (7%)
    all_gather x1, waiting for transfers between devices, local(): jax.lax.all_gather(table_acc, axis_name=('seq', 'dp')).sum(axis=0)  81.5 us
    ppermute x24, starting transfers between devices, from_partner(): return lax.ppermute(value, axis, pairs)  27.8 us
    ppermute x24, waiting for transfers between devices, from_partner(): return lax.ppermute(value, axis, pairs)  15.5 us
    dot_general x5, matrix products, grad_terms(): jnp.einsum('thd,uhd->htu', grad_heads, value_heads, preferred_element_typ...  11.6 us
    ppermute x8, local copies, waits for them, and re-layouts, from_partner(): return lax.ppermute(value, axis, pairs)  11.1 us
    dot_general x5, matrix products, local(): jnp.einsum('htu,uhd->thd', weights.astype(jnp.bfloat16), value_heads, pre...  10.9 us
    unnamed x26, local copies, waits for them, and re-layouts  9.96 us
    dot_general x5, matrix products, local(): jnp.einsum('htu,thd->uhd', probs_low, grad_heads, preferred_element_type=...  9.02 us
  transfers between devices with their start and end apart: 25, of which 7 were waited for; matrix products, arithmetic and copies ran while one was open for 28% of the time, Pallas kernels for 0%

profile of v1, /device:TPU:0, one launch (start us, length us, event | category | flops | bytes accessed | tf_op | source)
XLA Modules:
  0.0 239.8 jit_solution(3496753649328290169)
XLA Ops:
  8.0 4.0 %collective-permute-start.12 = (bf16[128]{0:T(256)(128)(2,1)S(1)}, bf16[128]{0:T(256)(128)(2,1)S(1)}, u32[]{:S(2)}, u32[]{:S(2)}) collective-permute-start(bf16[128]{0:T(256)(128)(2,1)S(1)} %get-tuple-element.45), channel_id=1, source_target_pairs={{0,16},{2,18},{4,20},{6,22},{8,24},{10,26},{12,28},{14,30},{16,0},... | collective-permute-start | bytes 776 | tf_op jit(solution)/shard_map/ppermute | solution.py:16
  24.2 1.8 collective-permute-start.10
  27.8 1.8 collective-permute-start.6
  32.9 2.6 %collective-permute-start.13 = (bf16[128,1024]{1,0:T(8,128)(2,1)}, bf16[128,1024]{1,0:T(8,128)(2,1)}, u32[]{:S(2)}, u32[]{:S(2)}) collective-permute-start(bf16[128,1024]{1,0:T(8,128)(2,1)} %bitcast.347), channel_id=1, source_target_pairs={{0,16},{2,18},{4,20},{6,22},{8,24},{10,26},{12,28},{14,30},{16,0},... | collective-permute-start | bytes 786440 | tf_op jit(solution)/shard_map/ppermute | solution.py:16
  39.1 2.7 %broadcast_compare_fusion = (pred[128,128]{0,1:T(8,128)(4,1)S(1)}, pred[128,128]{0,1:T(8,128)(4,1)S(1)}, pred[128,128]{0,1:T(8,128)(4,1)S(1)}, pred[128,128]{0,1:T(8,128)(4,1)S(1)}, pred[128,128]{0,1:T(8,128)(4,1)S(1)}) fusion(f32[128]{0:T(128)S(1)} %get-tuple-element.46, pred[]{:T(512)} %bitcast.25, f32[128]{0:T(128)S(1)} %convert_element_type.245, ...), kind=kLoop, calls=%fused_computation.151 | loop fusion | flops 147456 | bytes 84484 | tf_op jit(solution)/shard_map/eq | solution.py:43
  47.6 4.3 %collective-permute-done.9 = bf16[128,1024]{1,0:T(8,128)(2,1)} collective-permute-done((bf16[128,1024]{1,0:T(8,128)(2,1)}, bf16[128,1024]{1,0:T(8,128)(2,1)}, u32[]{:S(2)}, u32[]{:S(2)}) %collective-permute-start.9) | collective-permute-done | bytes 262176 | tf_op jit(solution)/shard_map/ppermute | solution.py:16
  53.7 2.4 fusion.151
  56.1 1.8 copy.119
  66.1 1.8 copy.114
  67.9 2.0 convolution_bitcast_fusion.2
  70.0 1.8 copy.117
  71.8 2.4 convolution_bitcast_fusion.1
  74.2 1.8 copy.120
  76.0 2.4 convolution_bitcast_fusion
  80.1 3.0 %multiply_reduce_fusion = (f32[128,16]{0,1:T(8,128)S(1)}, bf16[128,16,64]{0,2,1:T(8,128)(2,1)}) fusion(bf16[128,16,64]{0,2,1:T(8,128)(2,1)S(1)} %bitcast.301, f32[128,16]{0,1:T(8,128)} %get-tuple-element.20, f32[128,16,64]{0,2,1:T(8,128)} %convolution_bitcast_fusion, f32[128,16]{0,1:T(8,128)} %get-tuple-element.23, ...), kind=kOutput, calls=%fused_computation.103 | convolution fusion | flops 36042752 | bytes 3997696 | tf_op jit(solution)/shard_map/htu,uhd->thd/dot_general | solution.py:112
  83.2 2.6 %fusion.156 = (f32[16]{0:T(128)S(1)}, bf16[16,128,128]{1,2,0:T(8,128)(2,1)}) fusion(f32[16,128]{1,0:T(8,128)S(1)} %bitcast.363, bf16[128,16,64]{0,2,1:T(8,128)(2,1)S(1)} %bitcast.302, bf16[128,16,64]{0,2,1:T(8,128)(2,1)} %bitcast.357, f32[16,128,128]{1,2,0:T(8,128)} %get-tuple-element.54, f32[16,128]{1,0:T(8,128)S(1)} %log_add_fusion, ...), kind=kOutput, calls=%fused_computation.229 | convolution fusion | flops 35127280 | bytes 2129984 | tf_op jit(solution)/shard_map/thd,uhd->htu/dot_general | solution.py:57
  87.3 2.6 %fusion.158 = (f32[16]{0:T(128)S(1)}, bf16[16,128,128]{1,2,0:T(8,128)(2,1)}) fusion(f32[16,128]{1,0:T(8,128)S(1)} %bitcast.365, bf16[128,16,64]{0,2,1:T(8,128)(2,1)S(1)} %bitcast.304, bf16[128,16,64]{0,2,1:T(8,128)(2,1)} %bitcast.337, f32[16,128,128]{1,2,0:T(8,128)} %get-tuple-element.50, f32[16,128]{1,0:T(8,128)S(1)} %log_add_fusion, ...), kind=kOutput, calls=%fused_computation.231 | convolution fusion | flops 35127280 | bytes 2129984 | tf_op jit(solution)/shard_map/thd,uhd->htu/dot_general | solution.py:57
  89.9 2.6 %fusion.159 = (f32[16]{0:T(128)S(1)}, bf16[16,128,128]{1,2,0:T(8,128)(2,1)}) fusion(f32[16,128]{1,0:T(8,128)S(1)} %bitcast.366, bf16[128,16,64]{0,2,1:T(8,128)(2,1)S(1)} %bitcast.305, bf16[128,16,64]{0,2,1:T(8,128)(2,1)} %bitcast.339, f32[16,128,128]{1,2,0:T(8,128)} %copy-done.1, f32[16,128]{1,0:T(8,128)S(1)} %log_add_fusion, ...), kind=kOutput, calls=%fused_computation.232 | convolution fusion | flops 35127280 | bytes 2129984 | tf_op jit(solution)/shard_map/thd,uhd->htu/dot_general | solution.py:57
  92.5 2.2 fusion.155
  95.5 2.4 %multiply_add_fusion = f32[16,64,64]{2,1,0:T(8,128)} fusion(f32[64]{0:T(128)} %get-tuple-element.73, f32[16,64]{1,0:T(8,128)S(1)} %get-tuple-element.35, f32[64]{0:T(128)} %get-tuple-element.74, f32[16,64]{1,0:T(8,128)S(1)} %get-tuple-element.34, f32[64]{0:T(128)} %get-tuple-element.75, f32[16,64]{1,0:T(8,128)S(1)} %get-tuple-element.33, ...), kind=kLoop, calls=%fused_computation.102 | loop fusion | flops 589824 | bytes 283904 | tf_op jit(solution)/shard_map/add | solution.py:138
  98.0 2.5 %convolution_convert_fusion = bf16[16,128,64]{1,2,0:T(8,128)(2,1)} fusion(bf16[128,16,64]{0,2,1:T(8,128)(2,1)S(1)} %bitcast.307, f32[16,128,128]{1,2,0:T(8,128)} %copy-done.1, f32[16,128]{1,0:T(8,128)S(1)} %log_add_fusion, pred[128,128]{0,1:T(8,128)(4,1)S(1)} %get-tuple-element.39), kind=kOutput, calls=%fused_computation.56 | convolution fusion | flops 34471936 | bytes 1597440 | tf_op jit(solution)/shard_map/htu,thd->uhd/dot_general | solution.py:162
  100.5 2.4 %convolution_convert_fusion.1 = bf16[16,128,64]{1,2,0:T(8,128)(2,1)} fusion(bf16[128,16,64]{0,2,1:T(8,128)(2,1)S(1)} %bitcast.308, f32[16,128,128]{1,2,0:T(8,128)} %get-tuple-element.50, f32[16,128]{1,0:T(8,128)S(1)} %log_add_fusion, pred[128,128]{0,1:T(8,128)(4,1)S(1)} %get-tuple-element.38), kind=kOutput, calls=%fused_computation.57 | convolution fusion | flops 34471936 | bytes 1597440 | tf_op jit(solution)/shard_map/htu,thd->uhd/dot_general | solution.py:162
  105.3 2.5 %convolution_convert_fusion.3 = bf16[16,128,64]{1,2,0:T(8,128)(2,1)} fusion(bf16[128,16,64]{0,2,1:T(8,128)(2,1)S(1)} %bitcast.310, f32[16,128,128]{1,2,0:T(8,128)} %get-tuple-element.54, f32[16,128]{1,0:T(8,128)S(1)} %log_add_fusion, pred[128,128]{0,1:T(8,128)(4,1)S(1)} %get-tuple-element.40), kind=kOutput, calls=%fused_computation.59 | convolution fusion | flops 34471936 | bytes 1597440 | tf_op jit(solution)/shard_map/htu,thd->uhd/dot_general | solution.py:162
  108.0 2.2 fusion.29
  111.4 2.2 fusion.31
  120.4 1.8 copy.143
  123.1 1.8 collective-permute-start.18
  126.4 2.9 %collective-permute-start.19 = (bf16[128,1024]{0,1:T(8,128)(2,1)S(1)}, bf16[128,1024]{0,1:T(8,128)(2,1)S(1)}, u32[]{:S(2)}, u32[]{:S(2)}) collective-permute-start(bf16[128,1024]{0,1:T(8,128)(2,1)S(1)} %bitcast.361), channel_id=1, source_target_pairs={{0,16},{2,18},{4,20},{6,22},{8,24},{10,26},{12,28},{14,30},{16,0},... | collective-permute-start | bytes 786440 | tf_op jit(solution)/shard_map/ppermute | solution.py:16
  132.4 5.8 %collective-permute-done.18 = bf16[128,1024]{0,1:T(8,128)(2,1)S(1)} collective-permute-done((bf16[128,1024]{0,1:T(8,128)(2,1)}, bf16[128,1024]{0,1:T(8,128)(2,1)S(1)}, u32[]{:S(2)}, u32[]{:S(2)}) %collective-permute-start.18) | collective-permute-done | bytes 262176 | tf_op jit(solution)/shard_map/ppermute | solution.py:16
  138.2 3.5 %collective-permute-done.19 = bf16[128,1024]{0,1:T(8,128)(2,1)S(1)} collective-permute-done((bf16[128,1024]{0,1:T(8,128)(2,1)S(1)}, bf16[128,1024]{0,1:T(8,128)(2,1)S(1)}, u32[]{:S(2)}, u32[]{:S(2)}) %collective-permute-start.19) | collective-permute-done | bytes 262176 | tf_op jit(solution)/shard_map/ppermute | solution.py:16
  142.8 81.5 %all-gather.3.cloned.1.call-done = f32[512,64,64]{2,1,0:T(8,128)} async-done(((f32[16,64,64]{2,1,0:T(8,128)}), f32[512,64,64]{2,1,0:T(8,128)}) %all-gather.3.cloned.1.call-update) | async-done | bytes 8388624 | tf_op jit(solution)/shard_map/all_gather | solution.py:172
  224.3 8.7 %reduce_sum.134 = f32[16,64,64]{2,1,0:T(8,128)} reduce(f32[32,16,64,64]{3,2,1,0:T(8,128)} %bitcast.300, f32[]{:T(128)} %constant.8.clone.1), dimensions={0}, to_apply=%region_16.17 | reduce | flops 2031616 | bytes 8650756 | tf_op jit(solution)/shard_map/reduce_sum | solution.py:172
  (112 shorter events, 55.3 us)
Async XLA Ops:
  7.2 12.1 %copy-start = (bf16[16,64,64]{2,1,0:T(8,128)(2,1)S(1)}, bf16[16,64,64]{2,1,0:T(8,128)(2,1)}, u32[]{:S(2)}) copy-start(bf16[16,64,64]{2,1,0:T(8,128)(2,1)} %param.15) | copy-start | bytes 393220
  7.2 217.1 %all-gather.3.cloned.1.call-start = ((), (), s32[]{:S(2)}) async-start(), calls=%async_computation | async-start | bytes 17301504 | tf_op jit(solution)/shard_map/all_gather | solution.py:172
  8.0 28.9 %collective-permute-start.12 = (bf16[128]{0:T(256)(128)(2,1)S(1)}, bf16[128]{0:T(256)(128)(2,1)S(1)}, u32[]{:S(2)}, u32[]{:S(2)}) collective-permute-start(bf16[128]{0:T(256)(128)(2,1)S(1)} %get-tuple-element.45), channel_id=1, source_target_pairs={{0,16},{2,18},{4,20},{6,22},{8,24},{10,26},{12,28},{14,30},{16,0},... | collective-permute-start | bytes 776 | tf_op jit(solution)/shard_map/ppermute | solution.py:16
  12.0 25.4 %collective-permute-start.8 = (bf16[128]{0:T(256)(128)(2,1)S(1)}, bf16[128]{0:T(256)(128)(2,1)S(1)}, u32[]{:S(2)}, u32[]{:S(2)}) collective-permute-start(bf16[128]{0:T(256)(128)(2,1)S(1)} %get-tuple-element.45), channel_id=1, source_target_pairs={{0,8},{2,10},{4,12},{6,14},{8,0},{10,2},{12,4},{14,6},{16,24},{18,... | collective-permute-start | bytes 776 | tf_op jit(solution)/shard_map/ppermute | solution.py:16
  13.6 25.1 %collective-permute-start.4 = (bf16[128]{0:T(256)(128)(2,1)S(1)}, bf16[128]{0:T(256)(128)(2,1)S(1)}, u32[]{:S(2)}, u32[]{:S(2)}) collective-permute-start(bf16[128]{0:T(256)(128)(2,1)S(1)} %get-tuple-element.45), channel_id=1, source_target_pairs={{0,4},{2,6},{4,0},{6,2},{8,12},{10,14},{12,8},{14,10},{16,20},{18,... | collective-permute-start | bytes 776 | tf_op jit(solution)/shard_map/ppermute | solution.py:16
  15.1 23.6 %collective-permute-start = (bf16[128]{0:T(256)(128)(2,1)S(1)}, bf16[128]{0:T(256)(128)(2,1)S(1)}, u32[]{:S(2)}, u32[]{:S(2)}) collective-permute-start(bf16[128]{0:T(256)(128)(2,1)S(1)} %get-tuple-element.45), channel_id=1, source_target_pairs={{0,2},{2,0},{4,6},{6,4},{8,10},{10,8},{12,14},{14,12},{16,18},{18,... | collective-permute-start | bytes 776 | tf_op jit(solution)/shard_map/ppermute | solution.py:16
  15.8 8.5 %collective-permute-start.14 = (bf16[1]{0:T(256)(128)(2,1)}, bf16[1]{0:T(256)(128)(2,1)}, u32[]{:S(2)}, u32[]{:S(2)}) collective-permute-start(bf16[1]{0:T(256)(128)(2,1)} %bitcast.17), channel_id=1, source_target_pairs={{0,16},{2,18},{4,20},{6,22},{8,24},{10,26},{12,28},{14,30},{16,0},... | collective-permute-start | bytes 14 | tf_op jit(solution)/shard_map/ppermute | solution.py:16
  23.0 24.3 %copy-start.3 = (bf16[1,128,1024]{1,2,0:T(8,128)(2,1)}, bf16[1,128,1024]{1,2,0:T(8,128)(2,1)S(1)}, u32[]{:S(2)}) copy-start(bf16[1,128,1024]{1,2,0:T(8,128)(2,1)S(1)} %copy.107) | copy-start | bytes 786436
  24.2 59.0 %copy-start.4 = (bf16[1,128,1024]{1,2,0:T(8,128)(2,1)}, bf16[1,128,1024]{1,2,0:T(8,128)(2,1)S(1)}, u32[]{:S(2)}) copy-start(bf16[1,128,1024]{1,2,0:T(8,128)(2,1)S(1)} %copy.108) | copy-start | bytes 786436
  24.2 3.6 %collective-permute-start.10 = (bf16[1]{0:T(256)(128)(2,1)}, bf16[1]{0:T(256)(128)(2,1)}, u32[]{:S(2)}, u32[]{:S(2)}) collective-permute-start(bf16[1]{0:T(256)(128)(2,1)} %bitcast.17), channel_id=1, source_target_pairs={{0,8},{2,10},{4,12},{6,14},{8,0},{10,2},{12,4},{14,6},{16,24},{18,... | collective-permute-start | bytes 14 | tf_op jit(solution)/shard_map/ppermute | solution.py:16
  27.8 3.5 %collective-permute-start.6 = (bf16[1]{0:T(256)(128)(2,1)}, bf16[1]{0:T(256)(128)(2,1)}, u32[]{:S(2)}, u32[]{:S(2)}) collective-permute-start(bf16[1]{0:T(256)(128)(2,1)} %bitcast.17), channel_id=1, source_target_pairs={{0,4},{2,6},{4,0},{6,2},{8,12},{10,14},{12,8},{14,10},{16,20},{18,... | collective-permute-start | bytes 14 | tf_op jit(solution)/shard_map/ppermute | solution.py:16
  31.3 1.6 collective-permute-start.2
  32.9 23.2 %collective-permute-start.13 = (bf16[128,1024]{1,0:T(8,128)(2,1)}, bf16[128,1024]{1,0:T(8,128)(2,1)}, u32[]{:S(2)}, u32[]{:S(2)}) collective-permute-start(bf16[128,1024]{1,0:T(8,128)(2,1)} %bitcast.347), channel_id=1, source_target_pairs={{0,16},{2,18},{4,20},{6,22},{8,24},{10,26},{12,28},{14,30},{16,0},... | collective-permute-start | bytes 786440 | tf_op jit(solution)/shard_map/ppermute | solution.py:16
  36.8 15.1 %collective-permute-start.9 = (bf16[128,1024]{1,0:T(8,128)(2,1)}, bf16[128,1024]{1,0:T(8,128)(2,1)}, u32[]{:S(2)}, u32[]{:S(2)}) collective-permute-start(bf16[128,1024]{1,0:T(8,128)(2,1)} %bitcast.348), channel_id=1, source_target_pairs={{0,8},{2,10},{4,12},{6,14},{8,0},{10,2},{12,4},{14,6},{16,24},{18,... | collective-permute-start | bytes 786440 | tf_op jit(solution)/shard_map/ppermute | solution.py:16
  37.4 8.4 %collective-permute-start.5 = (bf16[128,1024]{1,0:T(8,128)(2,1)}, bf16[128,1024]{1,0:T(8,128)(2,1)S(1)}, u32[]{:S(2)}, u32[]{:S(2)}) collective-permute-start(bf16[128,1024]{1,0:T(8,128)(2,1)} %bitcast.349), channel_id=1, source_target_pairs={{0,4},{2,6},{4,0},{6,2},{8,12},{10,14},{12,8},{14,10},{16,20},{18,... | collective-permute-start | bytes 786440 | tf_op jit(solution)/shard_map/ppermute | solution.py:16
  38.7 3.5 %collective-permute-start.1 = (bf16[128,1024]{1,0:T(8,128)(2,1)}, bf16[128,1024]{1,0:T(8,128)(2,1)S(1)}, u32[]{:S(2)}, u32[]{:S(2)}) collective-permute-start(bf16[128,1024]{1,0:T(8,128)(2,1)} %bitcast.350), channel_id=1, source_target_pairs={{0,2},{2,0},{4,6},{6,4},{8,10},{10,8},{12,14},{14,12},{16,18},{18,... | collective-permute-start | bytes 786440 | tf_op jit(solution)/shard_map/ppermute | solution.py:16
  38.7 35.5 %collective-permute-start.15 = (bf16[128,1024]{1,0:T(8,128)(2,1)}, bf16[128,1024]{1,0:T(8,128)(2,1)}, u32[]{:S(2)}, u32[]{:S(2)}) collective-permute-start(bf16[128,1024]{1,0:T(8,128)(2,1)} %bitcast.351), channel_id=1, source_target_pairs={{0,16},{2,18},{4,20},{6,22},{8,24},{10,26},{12,28},{14,30},{16,0},... | collective-permute-start | bytes 786440 | tf_op jit(solution)/shard_map/ppermute | solution.py:16
  42.2 27.8 %collective-permute-start.11 = (bf16[128,1024]{1,0:T(8,128)(2,1)}, bf16[128,1024]{1,0:T(8,128)(2,1)}, u32[]{:S(2)}, u32[]{:S(2)}) collective-permute-start(bf16[128,1024]{1,0:T(8,128)(2,1)} %bitcast.352), channel_id=1, source_target_pairs={{0,8},{2,10},{4,12},{6,14},{8,0},{10,2},{12,4},{14,6},{16,24},{18,... | collective-permute-start | bytes 786440 | tf_op jit(solution)/shard_map/ppermute | solution.py:16
  45.8 20.3 %collective-permute-start.7 = (bf16[128,1024]{1,0:T(8,128)(2,1)}, bf16[128,1024]{1,0:T(8,128)(2,1)}, u32[]{:S(2)}, u32[]{:S(2)}) collective-permute-start(bf16[128,1024]{1,0:T(8,128)(2,1)} %bitcast.353), channel_id=1, source_target_pairs={{0,4},{2,6},{4,0},{6,2},{8,12},{10,14},{12,8},{14,10},{16,20},{18,... | collective-permute-start | bytes 786440 | tf_op jit(solution)/shard_map/ppermute | solution.py:16
  47.2 36.0 %copy-start.6 = (bf16[128,1024]{0,1:T(8,128)(2,1)}, bf16[128,1024]{0,1:T(8,128)(2,1)S(1)}, u32[]{:S(2)}) copy-start(bf16[128,1024]{0,1:T(8,128)(2,1)S(1)} %copy.113) | copy-start | bytes 786436
  51.9 26.4 %collective-permute-start.3 = (bf16[128,1024]{1,0:T(8,128)(2,1)}, bf16[128,1024]{1,0:T(8,128)(2,1)}, u32[]{:S(2)}, u32[]{:S(2)}) collective-permute-start(bf16[128,1024]{1,0:T(8,128)(2,1)} %bitcast.354), channel_id=1, source_target_pairs={{0,2},{2,0},{4,6},{6,4},{8,10},{10,8},{12,14},{14,12},{16,18},{18,... | collective-permute-start | bytes 786440 | tf_op jit(solution)/shard_map/ppermute | solution.py:16
  56.1 7.6 %copy-start.8 = (f32[16,128]{1,0:T(8,128)}, f32[16,128]{1,0:T(8,128)S(1)}, u32[]{:S(2)}) copy-start(f32[16,128]{1,0:T(8,128)S(1)} %get-tuple-element.49) | copy-start | bytes 24580
  98.0 21.7 %copy-start.7 = (bf16[128,1024]{0,1:T(8,128)(2,1)S(1)}, bf16[128,1024]{0,1:T(8,128)(2,1)}, u32[]{:S(2)}) copy-start(bf16[128,1024]{0,1:T(8,128)(2,1)} %copy-done.6) | copy-start | bytes 786436
  98.0 22.0 %copy-start.2 = (bf16[16,128,128]{1,2,0:T(8,128)(2,1)S(1)}, bf16[16,128,128]{1,2,0:T(8,128)(2,1)}, u32[]{:S(2)}) copy-start(bf16[16,128,128]{1,2,0:T(8,128)(2,1)} %get-tuple-element.68) | copy-start | bytes 1572868
  100.5 25.9 %collective-permute-start.23 = (bf16[128,1024]{0,1:T(8,128)(2,1)}, bf16[128,1024]{0,1:T(8,128)(2,1)}, u32[]{:S(2)}, u32[]{:S(2)}) collective-permute-start(bf16[128,1024]{0,1:T(8,128)(2,1)} %bitcast.84), channel_id=1, source_target_pairs={{0,16},{2,18},{4,20},{6,22},{8,24},{10,26},{12,28},{14,30},{16,0},... | collective-permute-start | bytes 786440 | tf_op jit(solution)/shard_map/ppermute | solution.py:16
  102.9 26.4 %collective-permute-start.22 = (bf16[128,1024]{0,1:T(8,128)(2,1)}, bf16[128,1024]{0,1:T(8,128)(2,1)}, u32[]{:S(2)}, u32[]{:S(2)}) collective-permute-start(bf16[128,1024]{0,1:T(8,128)(2,1)} %bitcast.81), channel_id=1, source_target_pairs={{0,8},{2,10},{4,12},{6,14},{8,0},{10,2},{12,4},{14,6},{16,24},{18,... | collective-permute-start | bytes 786440 | tf_op jit(solution)/shard_map/ppermute | solution.py:16
  104.1 26.1 %collective-permute-start.21 = (bf16[128,1024]{0,1:T(8,128)(2,1)}, bf16[128,1024]{0,1:T(8,128)(2,1)}, u32[]{:S(2)}, u32[]{:S(2)}) collective-permute-start(bf16[128,1024]{0,1:T(8,128)(2,1)} %bitcast.78), channel_id=1, source_target_pairs={{0,4},{2,6},{4,0},{6,2},{8,12},{10,14},{12,8},{14,10},{16,20},{18,... | collective-permute-start | bytes 786440 | tf_op jit(solution)/shard_map/ppermute | solution.py:16
  107.8 22.4 %collective-permute-start.20 = (bf16[128,1024]{0,1:T(8,128)(2,1)}, bf16[128,1024]{0,1:T(8,128)(2,1)}, u32[]{:S(2)}, u32[]{:S(2)}) collective-permute-start(bf16[128,1024]{0,1:T(8,128)(2,1)} %bitcast.75), channel_id=1, source_target_pairs={{0,2},{2,0},{4,6},{6,4},{8,10},{10,8},{12,14},{14,12},{16,18},{18,... | collective-permute-start | bytes 786440 | tf_op jit(solution)/shard_map/ppermute | solution.py:16
  123.1 15.1 %collective-permute-start.18 = (bf16[128,1024]{0,1:T(8,128)(2,1)}, bf16[128,1024]{0,1:T(8,128)(2,1)S(1)}, u32[]{:S(2)}, u32[]{:S(2)}) collective-permute-start(bf16[128,1024]{0,1:T(8,128)(2,1)} %bitcast.360), channel_id=1, source_target_pairs={{0,8},{2,10},{4,12},{6,14},{8,0},{10,2},{12,4},{14,6},{16,24},{18,... | collective-permute-start | bytes 786440 | tf_op jit(solution)/shard_map/ppermute | solution.py:16
  126.4 15.4 %collective-permute-start.19 = (bf16[128,1024]{0,1:T(8,128)(2,1)S(1)}, bf16[128,1024]{0,1:T(8,128)(2,1)S(1)}, u32[]{:S(2)}, u32[]{:S(2)}) collective-permute-start(bf16[128,1024]{0,1:T(8,128)(2,1)S(1)} %bitcast.361), channel_id=1, source_target_pairs={{0,16},{2,18},{4,20},{6,22},{8,24},{10,26},{12,28},{14,30},{16,0},... | collective-permute-start | bytes 786440 | tf_op jit(solution)/shard_map/ppermute | solution.py:16
  129.3 12.4 %collective-permute-start.17 = (bf16[128,1024]{0,1:T(8,128)(2,1)}, bf16[128,1024]{0,1:T(8,128)(2,1)S(1)}, u32[]{:S(2)}, u32[]{:S(2)}) collective-permute-start(bf16[128,1024]{0,1:T(8,128)(2,1)} %bitcast.359), channel_id=1, source_target_pairs={{0,4},{2,6},{4,0},{6,2},{8,12},{10,14},{12,8},{14,10},{16,20},{18,... | collective-permute-start | bytes 786440 | tf_op jit(solution)/shard_map/ppermute | solution.py:16
  130.2 11.6 %collective-permute-start.16 = (bf16[128,1024]{0,1:T(8,128)(2,1)}, bf16[128,1024]{0,1:T(8,128)(2,1)S(1)}, u32[]{:S(2)}, u32[]{:S(2)}) collective-permute-start(bf16[128,1024]{0,1:T(8,128)(2,1)} %bitcast.358), channel_id=1, source_target_pairs={{0,2},{2,0},{4,6},{6,4},{8,10},{10,8},{12,14},{14,12},{16,18},{18,... | collective-permute-start | bytes 786440 | tf_op jit(solution)/shard_map/ppermute | solution.py:16
  (2 other events, 4.3 us)
Sparse Core Ops, SparseCore 0:
  98.1 126.1 all-gather.2
